TPU v7x, 32 devices: a whole 2x2x4 slice. The times are simulated.
32 devices in a mesh: row: 4 (over z), col: 4 (over y, x), vec: 2 (over core).
Axes of the slice: x: 2, y: 2, z: 4, core: 2. Of those that a mesh axis runs over, the one named last changes fastest.
Arguments:
- vectors: bfloat16 [8, 32768], P('vec', 'row'), may hold values from -6 to 6
- energy: float32 [32768], P('row'), may hold values from 1 to 10
- tiles: bfloat16 [4, 4, 192, 4096], P('row', 'col'), may hold values from -0.30618622 to 0.30618622
- tile_rows: int32 [4, 4, 192], P('row', 'col'), may hold values from 0 to 127
- tile_cols: int32 [4, 4, 192], P('row', 'col'), may hold values from 0 to 127
- counts: int32 [4, 4], P('row', 'col'), may hold values from 48 to 192, as said below
Outputs:
- image: float32 [8, 32768], P('vec', 'row')
- residual_image: float32 [8, 32768], P('vec', 'row')
Inputs may be any that keep to these rules, and one draw needn't show every extreme that they name: `counts`: at least one block has all 192 slots live in every draw; slots at or past a block's count hold no part of H.
All inputs are finite; a program needn't handle non-finite values.
Results may differ from a plain program's by a relative error of at most 0.004.
Values may be sent and summed in bfloat16 or wider, within the bound.
A program may use at most 64 MiB of HBM per device.

v0:
```python
import functools

import jax
import jax.numpy as jnp
from jax import lax
from jax.experimental import pallas as pl
from jax.experimental.pallas import tpu as pltpu
from jax.sharding import PartitionSpec as P

F32 = jnp.float32
BF16 = jnp.bfloat16
SIDE = 64
LANES = 128


def kernel(
    n, counts_ref, raw_any, e_any, rows_any, cols_any, t_any, image_out, second_out,
    raw_ref, e_ref, t_ref, rows_ref, cols_ref, v_ref, grid, image_ref, second_ref, spread_mat, low_mat, high_mat, prods, acc, near, far, row_part, row_stage, col_stage,
    row_in, col_in, num_out, num_in, far_send, far_recv, near_send, near_recv, row_send,
    row_recv, col_send, col_recv, num_send, num_recv, out_send, out_recv, load_sem,
):
    r, c = lax.axis_index("row"), lax.axis_index("col")
    me = r * n + c
    everyone = n * n
    pieces, depth, width = v_ref.shape
    groups = pieces * depth
    pairs = width // LANES
    slots, area = t_ref.shape
    diagonal = r == c

    def copy(src, dst, send, recv, row, col):
        return pltpu.make_async_remote_copy(
            src_ref=src, dst_ref=dst, send_sem=send, recv_sem=recv,
            device_id={"row": row, "col": col}, device_id_type=pl.DeviceIdType.MESH,
        )

    def each(start, stop, body):
        def step(i, carry):
            body(i)
            return carry

        lax.fori_loop(start, stop, step, 0)

    def far_copy(src, phase, shift):
        return copy(
            src, far.at[phase, c], far_send.at[phase, shift - 1], far_recv.at[phase, c],
            lax.rem(r + shift, n), r,
        )

    def far_wait(phase):
        @pl.when(jnp.logical_not(diagonal))
        def _():
            each(0, n, lambda q: copy(
                near.at[q], far.at[phase, q], far_send.at[phase, 0], far_recv.at[phase, q], r, c
            ).wait_recv())

    def row_copy(phase, shift):
        q = lax.rem(c + shift, n)
        return copy(
            row_stage.at[phase, q], row_in.at[phase, c], row_send.at[phase, shift - 1],
            row_recv.at[phase, c], r, q,
        )

    def col_copy(phase, q):
        return copy(
            col_stage.at[phase, q], col_in.at[phase, r], col_send.at[phase, q],
            col_recv.at[phase, r], c, q,
        )

    def not_me(q, body):
        @pl.when(jnp.logical_not(jnp.logical_and(diagonal, q == c)))
        def _():
            body()

    def near_copy(shift):
        return copy(
            near.at[c], near.at[c], near_send.at[shift - 1], near_recv.at[c],
            r, lax.rem(c + shift, n),
        )

    def out_copy(phase, ref, shift):
        return copy(
            ref.at[c], ref.at[c], out_send.at[phase, shift - 1], out_recv.at[phase, c],
            r, lax.rem(c + shift, n),
        )

    def num_copy(shift):
        peer = lax.rem(me + shift, everyone)
        return copy(
            num_out, num_in.at[me], num_send.at[shift - 1], num_recv.at[me],
            peer // n, lax.rem(peer, n),
        )

    barrier = pltpu.get_barrier_semaphore()

    def greet(shift):
        peer = lax.rem(me + shift, everyone)
        pl.semaphore_signal(
            barrier, inc=1, device_id={"row": peer // n, "col": lax.rem(peer, n)},
            device_id_type=pl.DeviceIdType.MESH,
        )

    loads = [
        pltpu.make_async_copy(src, dst, load_sem.at[i])
        for i, (src, dst) in enumerate(
            ((raw_any, raw_ref), (e_any, e_ref), (rows_any, rows_ref), (cols_any, cols_ref), (t_any, t_ref))
        )
    ]
    for load in loads:
        load.start()
    each(1, everyone, greet)

    for load in loads[:2]:
        load.wait()
    half_rows = groups // 2
    half_left = lax.broadcasted_iota(jnp.int32, (half_rows, LANES), 1) < SIDE
    for p in range(pairs):
        first, second = raw_ref[2 * p].astype(F32), raw_ref[2 * p + 1].astype(F32)
        grid[p, pl.ds(0, half_rows, stride=2), :] = jnp.where(
            half_left, first, pltpu.roll(second, SIDE, 1)
        )
        grid[p, pl.ds(1, half_rows, stride=2), :] = jnp.where(
            half_left, pltpu.roll(first, SIDE, 1), second
        )
    for p in range(pairs):
        v_ref[:, :, LANES * p: LANES * (p + 1)] = (
            grid[p].reshape(pieces, depth, LANES).astype(BF16)
        )
    energies = e_ref[...]
    turned = pltpu.roll(energies, SIDE, 1)
    grid[0, pl.ds(0, half_rows, stride=2), :] = jnp.where(half_left, energies, turned)
    grid[0, pl.ds(1, half_rows, stride=2), :] = jnp.where(half_left, turned, energies)
    energy = grid[0, pl.ds(pl.multiple_of(c * depth, depth), depth), :]
    energy = jnp.concatenate([energy] * pairs, axis=1)

    shift = SIDE.bit_length() - 1
    spread_mat[...] = (
        lax.shift_right_logical(lax.broadcasted_iota(jnp.int32, spread_mat.shape, 0), shift)
        == lax.broadcasted_iota(jnp.int32, spread_mat.shape, 1)
    ).astype(BF16)
    owner = lax.shift_right_logical(lax.broadcasted_iota(jnp.int32, low_mat.shape, 1), shift)
    line = lax.broadcasted_iota(jnp.int32, low_mat.shape, 0)
    low_mat[...] = (owner == line).astype(BF16)
    high_mat[...] = (owner + SIDE == line).astype(BF16)

    pl.semaphore_wait(barrier, everyone - 1)
    each(1, n, lambda s: far_copy(v_ref.at[c], 0, s).start())
    for load in loads[2:]:
        load.wait()

    live = lax.broadcasted_iota(jnp.int32, (groups, slots), 1) < counts_ref[0, 0]
    place = lax.broadcasted_iota(jnp.int32, (groups, slots), 0)
    pick_rows = jnp.where(jnp.logical_and(place == rows_ref[...], live), 1.0, 0.0).astype(BF16)
    pick_cols = jnp.where(jnp.logical_and(place == cols_ref[...], live), 1.0, 0.0).astype(BF16)
    left = lax.broadcasted_iota(jnp.int32, (slots, LANES), 1) < SIDE

    def whole(value):
        return value.astype(F32).reshape(groups, width).astype(BF16)

    def fetch(pick, value):
        return lax.dot_general(
            pick, whole(value), (((0,), (0,)), ((), ())), preferred_element_type=F32
        )

    def deposit(pick, value):
        upper = value.astype(BF16)
        lower = (value - upper.astype(F32)).astype(BF16)
        total = jnp.dot(pick, upper, preferred_element_type=F32) + jnp.dot(
            pick, lower, preferred_element_type=F32
        )
        return total.reshape(pieces, depth, width)

    def backward(own):
        mine = fetch(pick_rows, own)
        stacked = jnp.concatenate(
            [mine[:, LANES * p: LANES * (p + 1)] for p in range(pairs)], axis=0
        ).astype(BF16)
        acc[...] = jnp.zeros_like(acc)
        chunk = 4 * LANES

        def step(i, carry):
            at = pl.ds(pl.multiple_of(i * chunk, chunk), chunk)
            tile = t_ref[:, at].astype(F32)
            for half, mat in enumerate((low_mat, high_mat)):
                wide = jnp.dot(stacked, mat[:, at], preferred_element_type=F32)
                for p in range(pairs):
                    prod = wide[slots * p: slots * (p + 1)] * tile
                    part = prod[:, :LANES]
                    for j in range(1, chunk // LANES):
                        part = part + prod[:, LANES * j: LANES * (j + 1)]
                    acc[2 * p + half] += part
            return carry

        lax.fori_loop(0, area // chunk, step, 0, unroll=2)
        parts = []
        for p in range(pairs):
            first, second = acc[2 * p], acc[2 * p + 1]
            parts.append(jnp.where(
                left, first + pltpu.roll(first, SIDE, 1), second + pltpu.roll(second, SIDE, 1)
            ))
        return jnp.concatenate(parts, axis=1)

    def forward(theirs):
        twins = []
        for p in range(pairs):
            both = theirs[:, LANES * p: LANES * (p + 1)]
            turned = pltpu.roll(both, SIDE, 1)
            for twin in (jnp.where(left, both, turned), jnp.where(left, turned, both)):
                twins.append(jnp.concatenate([twin.astype(BF16)] * 8, axis=1))

        chunk = 8 * LANES
        prods[...] = jnp.zeros_like(prods)

        def step(i, carry):
            base = pl.multiple_of(i * chunk, chunk)
            tile = t_ref[:, pl.ds(base, chunk)]
            total = None
            for half in range(2):
                left_side = jnp.concatenate(
                    [tile * twins[2 * p + half] for p in range(pairs)], axis=0
                )
                start = pl.multiple_of(base + half * area, chunk)
                part = jnp.dot(
                    left_side, spread_mat[pl.ds(start, chunk), :], preferred_element_type=F32
                )
                total = part if total is None else total + part
            prods[...] += total
            return carry

        lax.fori_loop(0, area // chunk, step, 0, unroll=2)
        summed = prods[...]
        return jnp.concatenate(
            [summed[slots * p: slots * (p + 1)] for p in range(pairs)], axis=1
        )

    def scatter_col(phase, part):
        col_stage[phase] = part.astype(BF16)
        each(0, n, lambda q: not_me(q, lambda: col_copy(phase, q).start()))

        @pl.when(diagonal)
        def _():
            col_in[phase, r] = col_stage[phase, c]

    def scatter_row(phase, part):
        row_part[...] = part
        row_stage[phase] = part.astype(BF16)
        each(1, n, lambda s: row_copy(phase, s).start())

    def gathered(phase, start):
        def row_step(s, carry):
            q = lax.rem(c + s, n)
            copy(
                row_stage.at[phase, 0], row_in.at[phase, q], row_send.at[phase, 0],
                row_recv.at[phase, q], r, q,
            ).wait_recv()
            return carry + row_in[phase, q].astype(F32)

        total = lax.fori_loop(1, n, row_step, start + row_part[c])

        def col_step(q, carry):
            @pl.when(jnp.logical_not(jnp.logical_and(diagonal, q == r)))
            def _():
                copy(
                    col_stage.at[phase, 0], col_in.at[phase, q], col_send.at[phase, 0],
                    col_recv.at[phase, q], q, r,
                ).wait_recv()

            return carry + col_in[phase, q].astype(F32)

        return lax.fori_loop(0, n, col_step, total)

    sums_back = backward(v_ref[...])
    scatter_col(0, deposit(pick_cols, sums_back))
    far_wait(0)

    @pl.when(diagonal)
    def _():
        far[0] = v_ref[...]

    theirs = fetch(pick_cols, far[0])
    block = v_ref[c].astype(F32)
    weighted = energy * block
    top = 2.0 * jnp.sum(theirs * sums_back, axis=0, keepdims=True) + jnp.sum(
        weighted * block, axis=0, keepdims=True
    )
    bottom = jnp.sum(block * block, axis=0, keepdims=True)
    lane = lax.broadcasted_iota(jnp.int32, num_out.shape, 1)
    odd = jnp.bitwise_and(lane, 1) == 1
    shift = SIDE // 2
    while shift:
        lower = jnp.bitwise_and(lane, shift) == 0
        top, bottom = (
            x + jnp.where(lower, pltpu.roll(x, width - shift, 1), pltpu.roll(x, shift, 1))
            for x in (top, bottom)
        )
        shift //= 2
    num_out[...] = jnp.where(odd, bottom, top)
    num_in[me] = num_out[...]
    each(1, everyone, lambda s: num_copy(s).start())

    scatter_row(0, deposit(pick_rows, forward(theirs)))
    image = gathered(0, weighted)
    image_ref[c] = image

    def num_step(s, carry):
        peer = lax.rem(me + s, everyone)
        copy(
            num_out, num_in.at[peer], num_send.at[0], num_recv.at[peer], r, c
        ).wait_recv()
        return carry

    lax.fori_loop(1, everyone, num_step, 0)
    sums = lax.fori_loop(
        0, everyone, lambda i, total: total + num_in[i], jnp.zeros(num_out.shape, F32)
    )
    after = pltpu.roll(sums, width - 1, 1)
    before = pltpu.roll(sums, 1, 1)
    theta = jnp.where(odd, before, sums) / jnp.where(odd, sums, after)
    residual = (image - theta * block).astype(BF16)
    near[c] = residual
    each(1, n, lambda s: far_copy(near.at[c], 1, s).start())
    each(1, n, lambda s: near_copy(s).start())

    def near_wait(s):
        q = lax.rem(c + s, n)
        copy(near.at[q], near.at[q], near_send.at[0], near_recv.at[q], r, c).wait_recv()

    each(1, n, near_wait)
    each(1, n, lambda s: out_copy(0, image_ref, s).start())
    scatter_col(1, deposit(pick_cols, backward(near[...])))
    far_wait(1)

    @pl.when(diagonal)
    def _():
        far[1] = near[...]

    scatter_row(1, deposit(pick_rows, forward(fetch(pick_cols, far[1]))))
    def emit(ref, out):
        for p in range(pairs):
            grid[p] = ref[:, :, LANES * p: LANES * (p + 1)].reshape(groups, LANES)
        for p in range(pairs):
            even = grid[p, pl.ds(0, half_rows, stride=2), :]
            odds = grid[p, pl.ds(1, half_rows, stride=2), :]
            out[2 * p] = jnp.where(half_left, even, pltpu.roll(odds, SIDE, 1))
            out[2 * p + 1] = jnp.where(half_left, pltpu.roll(even, SIDE, 1), odds)

    def out_wait(phase, ref, s):
        q = lax.rem(c + s, n)
        copy(
            ref.at[q], ref.at[q], out_send.at[phase, 0], out_recv.at[phase, q], r, c
        ).wait_recv()

    each(1, n, lambda s: out_wait(0, image_ref, s))
    emit(image_ref, image_out)
    second_ref[c] = gathered(1, energy * residual.astype(F32))
    each(1, n, lambda s: out_copy(1, second_ref, s).start())

    def finish(s):
        out_wait(1, second_ref, s)
        for phase, ref in enumerate((image_ref, second_ref)):
            out_copy(phase, ref, s).wait_send()
            row_copy(phase, s).wait_send()
        far_copy(v_ref.at[c], 0, s).wait_send()
        far_copy(near.at[c], 1, s).wait_send()
        near_copy(s).wait_send()

    each(1, n, finish)

    emit(second_ref, second_out)
    for phase in range(2):
        each(0, n, lambda q: not_me(q, lambda: col_copy(phase, q).wait_send()))
    each(1, everyone, lambda s: num_copy(s).wait_send())


def local(n, vectors, energy, tiles, tile_rows, tile_cols, counts):
    here, group_width = vectors.shape
    groups = group_width // SIDE
    width = here * SIDE
    depth = groups // n
    slots, area = tiles.shape[2:]
    everyone = n * n
    pairs = width // LANES
    half_rows = groups // 2
    vmem = pl.BlockSpec(memory_space=pltpu.VMEM)
    hbm = pl.BlockSpec(memory_space=pltpu.HBM)
    dma = pltpu.SemaphoreType.DMA
    image, second = pl.pallas_call(
        functools.partial(kernel, n),
        out_shape=[jax.ShapeDtypeStruct((here, half_rows, LANES), F32)] * 2,
        in_specs=[pl.BlockSpec(memory_space=pltpu.SMEM)] + [hbm] * 5,
        out_specs=[vmem, vmem],
        scratch_shapes=[
            pltpu.VMEM((here, half_rows, LANES), BF16),
            pltpu.VMEM((half_rows, LANES), F32),
            pltpu.VMEM((slots, area), BF16),
            pltpu.VMEM((1, slots), jnp.int32),
            pltpu.VMEM((1, slots), jnp.int32),
            pltpu.VMEM((n, depth, width), BF16),
            pltpu.VMEM((pairs, groups, LANES), F32),
            pltpu.VMEM((n, depth, width), F32),
            pltpu.VMEM((n, depth, width), F32),
            pltpu.VMEM((2 * area, LANES), BF16),
            pltpu.VMEM((LANES, area), BF16),
            pltpu.VMEM((LANES, area), BF16),
            pltpu.VMEM((pairs * slots, LANES), F32),
            pltpu.VMEM((2 * pairs, slots, LANES), F32),
            pltpu.VMEM((n, depth, width), BF16),
            pltpu.VMEM((2, n, depth, width), BF16),
            pltpu.VMEM((n, depth, width), F32),
            pltpu.VMEM((2, n, depth, width), BF16),
            pltpu.VMEM((2, n, depth, width), BF16),
            pltpu.VMEM((2, n, depth, width), BF16),
            pltpu.VMEM((2, n, depth, width), BF16),
            pltpu.VMEM((1, width), F32),
            pltpu.VMEM((everyone, 1, width), F32),
            dma((2, n)), dma((2, n)), dma((n,)), dma((n,)), dma((2, n)), dma((2, n)),
            dma((2, n)), dma((2, n)), dma((everyone,)), dma((everyone,)), dma((2, n)), dma((2, n)),
            dma((5,)),
        ],
        compiler_params=pltpu.CompilerParams(
            collective_id=0, has_side_effects=True, vmem_limit_bytes=67043328
        ),
    )(
        counts, vectors.reshape(here, half_rows, LANES), energy.reshape(half_rows, LANES),
        tile_rows[0], tile_cols[0], tiles[0, 0],
    )

    return image.reshape(here, group_width), second.reshape(here, group_width)


def solution(mesh):
    in_specs = (
        P("vec", "row"),
        P("row"),
        P("row", "col", None, None),
        P("row", "col", None),
        P("row", "col", None),
        P("row", "col"),
    )
    out_specs = (P("vec", "row"), P("vec", "row"))
    return jax.shard_map(
        functools.partial(local, mesh.shape["row"]), mesh=mesh, in_specs=in_specs,
        out_specs=out_specs, check_vma=False,
    )
```

profile of v0, /device:TPU:0, one launch (start us, length us, event | category | flops | bytes accessed | tf_op | source)
XLA Modules:
  0.0 39.4 jit_solution(14107174511306276220)
XLA Ops:
  1.3 1.5 %copy.14 = bf16[1,4,64,128]{3,2,1,0:T(8,128)(2,1)} copy(bf16[1,4,64,128]{3,1,2,0:T(4,128)(2,1)} %bitcast.18) | data formatting | bytes 131072
  2.8 34.8 %shard_map.77 = (f32[4,64,128]{2,1,0:T(8,128)}, f32[4,64,128]{2,1,0:T(8,128)}) custom-call(s32[1,1]{1,0:T(1,128)S(6)} %copy.15.counts_ref, bf16[4,64,128]{2,1,0:T(8,128)(2,1)} %bitcast.15, f32[64,128]{1,0:T(8,128)} %bitcast.19, s32[1,192]{1,0:T(1,128)} %bitcast.20, s32[1,192]{1,0:T(1,128)} %bitcast.21, bf16[192,4096]{1,0:T(8,128)(2,1)} %bitcast.14), custom_call_target="tpu_custom_call" | custom-call | tf_op jit(solution)/shard_map/pallas_call | solution.py:387
  37.5 1.8 %copy_bitcast_fusion = (f32[4,8192]{1,0:T(4,128)}, f32[4,8192]{1,0:T(4,128)}) fusion(f32[1,4,64,128]{3,2,1,0:T(8,128)} %bitcast.17, f32[1,4,64,128]{3,2,1,0:T(8,128)} %bitcast.16), kind=kLoop, calls=%fused_computation | loop fusion | bytes 524288 | tf_op jit(solution)/shard_map/reshape | solution.py:428
where the time goes:
time: 39.6 us; the launch traced here: 39.4 us
  Pallas kernels  34.8 us (88%)
  local copies, waits for them, and re-layouts  3.32 us (8%)
  between operations  1.28 us (3%)
    pallas_call x1, Pallas kernels, local(): pl.pallas_call(functools.partial(kernel, n), out_shape=[jax.ShapeDtypeStr...  34.8 us
    reshape x1, local copies, waits for them, and re-layouts, local(): return (image.reshape(here, group_width), second.reshape(here, group_width))  1.84 us
    unnamed x1, local copies, waits for them, and re-layouts  1.48 us

commit v1 on v0

--- a/solution.py
+++ b/solution.py
@@ -15,7 +15,7 @@
 
 def kernel(
     n, counts_ref, raw_any, e_any, rows_any, cols_any, t_any, image_out, second_out,
-    raw_ref, e_ref, t_ref, rows_ref, cols_ref, v_ref, grid, image_ref, second_ref, spread_mat, low_mat, high_mat, prods, acc, near, far, row_part, row_stage, col_stage,
+    raw_ref, e_ref, t_ref, rows_ref, cols_ref, v_ref, wide, final, spread_mat, low_mat, high_mat, prods, acc, near, far, row_part, row_stage, col_stage,
     row_in, col_in, num_out, num_in, far_send, far_recv, near_send, near_recv, row_send,
     row_recv, col_send, col_recv, num_send, num_recv, out_send, out_recv, load_sem,
 ):
@@ -78,10 +78,15 @@
             r, lax.rem(c + shift, n),
         )
 
+    block_rows = final.shape[1]
+
+    def lines(ref, q):
+        return ref.at[pl.ds(pl.multiple_of(q * block_rows, block_rows), block_rows), :]
+
     def out_copy(phase, ref, shift):
         return copy(
-            ref.at[c], ref.at[c], out_send.at[phase, shift - 1], out_recv.at[phase, c],
-            r, lax.rem(c + shift, n),
+            final.at[phase], lines(ref, c), out_send.at[phase, shift - 1],
+            out_recv.at[phase, c], r, lax.rem(c + shift, n),
         )
 
     def num_copy(shift):
@@ -103,7 +108,10 @@
     loads = [
         pltpu.make_async_copy(src, dst, load_sem.at[i])
         for i, (src, dst) in enumerate(
-            ((raw_any, raw_ref), (e_any, e_ref), (rows_any, rows_ref), (cols_any, cols_ref), (t_any, t_ref))
+            (
+                (raw_any, raw_ref), (e_any, e_ref), (rows_any, rows_ref), (cols_any, cols_ref),
+                (t_any, t_ref),
+            )
         )
     ]
     for load in loads:
@@ -112,46 +120,57 @@
 
     for load in loads[:2]:
         load.wait()
+    here = width // SIDE
     half_rows = groups // 2
-    half_left = lax.broadcasted_iota(jnp.int32, (half_rows, LANES), 1) < SIDE
+    half = depth // 2
+
+    def pack(parts):
+        out = []
+        for p in range(len(parts) // 2):
+            first, second = parts[2 * p], parts[2 * p + 1]
+            mask = lax.broadcasted_iota(jnp.int32, first.shape, 1) < SIDE
+            out.append((
+                jnp.where(mask, first, pltpu.roll(second, SIDE, 1)),
+                jnp.where(mask, pltpu.roll(first, SIDE, 1), second),
+            ))
+        return out
+
+    wide[...] = raw_ref[...].astype(F32)
+    packed = pack([wide[pl.ds(k, half_rows, stride=here), :] for k in range(here)])
     for p in range(pairs):
-        first, second = raw_ref[2 * p].astype(F32), raw_ref[2 * p + 1].astype(F32)
-        grid[p, pl.ds(0, half_rows, stride=2), :] = jnp.where(
-            half_left, first, pltpu.roll(second, SIDE, 1)
-        )
-        grid[p, pl.ds(1, half_rows, stride=2), :] = jnp.where(
-            half_left, pltpu.roll(first, SIDE, 1), second
-        )
-    for p in range(pairs):
-        v_ref[:, :, LANES * p: LANES * (p + 1)] = (
-            grid[p].reshape(pieces, depth, LANES).astype(BF16)
-        )
-    energies = e_ref[...]
-    turned = pltpu.roll(energies, SIDE, 1)
-    grid[0, pl.ds(0, half_rows, stride=2), :] = jnp.where(half_left, energies, turned)
-    grid[0, pl.ds(1, half_rows, stride=2), :] = jnp.where(half_left, turned, energies)
-    energy = grid[0, pl.ds(pl.multiple_of(c * depth, depth), depth), :]
-    energy = jnp.concatenate([energy] * pairs, axis=1)
+        for parity in range(2):
+            for q in range(pieces):
+                v_ref[q, half * parity: half * (parity + 1), LANES * p: LANES * (p + 1)] = (
+                    packed[p][parity][half * q: half * (q + 1)].astype(BF16)
+                )
+    energies = e_ref[pl.ds(pl.multiple_of(c * half, half), half), :]
+    ((upper_energy, lower_energy),) = pack([energies, energies])
+    energy = jnp.concatenate(
+        [jnp.concatenate([upper_energy, lower_energy], axis=0)] * pairs, axis=1
+    )
 
     shift = SIDE.bit_length() - 1
-    spread_mat[...] = (
-        lax.shift_right_logical(lax.broadcasted_iota(jnp.int32, spread_mat.shape, 0), shift)
-        == lax.broadcasted_iota(jnp.int32, spread_mat.shape, 1)
-    ).astype(BF16)
     owner = lax.shift_right_logical(lax.broadcasted_iota(jnp.int32, low_mat.shape, 1), shift)
     line = lax.broadcasted_iota(jnp.int32, low_mat.shape, 0)
     low_mat[...] = (owner == line).astype(BF16)
     high_mat[...] = (owner + SIDE == line).astype(BF16)
 
-    pl.semaphore_wait(barrier, everyone - 1)
-    each(1, n, lambda s: far_copy(v_ref.at[c], 0, s).start())
     for load in loads[2:]:
         load.wait()
 
     live = lax.broadcasted_iota(jnp.int32, (groups, slots), 1) < counts_ref[0, 0]
     place = lax.broadcasted_iota(jnp.int32, (groups, slots), 0)
-    pick_rows = jnp.where(jnp.logical_and(place == rows_ref[...], live), 1.0, 0.0).astype(BF16)
-    pick_cols = jnp.where(jnp.logical_and(place == cols_ref[...], live), 1.0, 0.0).astype(BF16)
+
+    def home(index):
+        inside = jnp.bitwise_and(index, depth - 1)
+        return index - inside + half * jnp.bitwise_and(index, 1) + lax.shift_right_logical(inside, 1)
+
+    pick_rows = jnp.where(
+        jnp.logical_and(place == home(rows_ref[...]), live), 1.0, 0.0
+    ).astype(BF16)
+    pick_cols = jnp.where(
+        jnp.logical_and(place == home(cols_ref[...]), live), 1.0, 0.0
+    ).astype(BF16)
     left = lax.broadcasted_iota(jnp.int32, (slots, LANES), 1) < SIDE
 
     def whole(value):
@@ -269,8 +288,17 @@
 
         return lax.fori_loop(0, n, col_step, total)
 
+    pl.semaphore_wait(barrier, everyone - 1)
+    each(1, n, lambda s: far_copy(v_ref.at[c], 0, s).start())
     sums_back = backward(v_ref[...])
-    scatter_col(0, deposit(pick_cols, sums_back))
+    col_part = deposit(pick_cols, sums_back)
+    scatter_col(0, col_part)
+    spread_mat[...] = (
+        lax.shift_right_logical(
+            lax.broadcasted_iota(jnp.int32, spread_mat.shape, 0), SIDE.bit_length() - 1
+        )
+        == lax.broadcasted_iota(jnp.int32, spread_mat.shape, 1)
+    ).astype(BF16)
     far_wait(0)
 
     @pl.when(diagonal)
@@ -299,8 +327,18 @@
     each(1, everyone, lambda s: num_copy(s).start())
 
     scatter_row(0, deposit(pick_rows, forward(theirs)))
+    def publish(phase, ref, block):
+        parts = []
+        for p in range(pairs):
+            lanes = block[:, LANES * p: LANES * (p + 1)]
+            parts.append((lanes[:half], lanes[half:]))
+        for p in range(pairs):
+            (turned,) = pack(list(parts[p]))
+            for i in range(2):
+                final[phase, pl.ds(2 * p + i, half, stride=here), :] = turned[i]
+        lines(ref, c)[...] = final[phase]
+
     image = gathered(0, weighted)
-    image_ref[c] = image
 
     def num_step(s, carry):
         peer = lax.rem(me + s, everyone)
@@ -325,8 +363,9 @@
         q = lax.rem(c + s, n)
         copy(near.at[q], near.at[q], near_send.at[0], near_recv.at[q], r, c).wait_recv()
 
+    publish(0, image_out, image)
     each(1, n, near_wait)
-    each(1, n, lambda s: out_copy(0, image_ref, s).start())
+    each(1, n, lambda s: out_copy(0, image_out, s).start())
     scatter_col(1, deposit(pick_cols, backward(near[...])))
     far_wait(1)
 
@@ -335,41 +374,44 @@
         far[1] = near[...]
 
     scatter_row(1, deposit(pick_rows, forward(fetch(pick_cols, far[1]))))
-    def emit(ref, out):
-        for p in range(pairs):
-            grid[p] = ref[:, :, LANES * p: LANES * (p + 1)].reshape(groups, LANES)
-        for p in range(pairs):
-            even = grid[p, pl.ds(0, half_rows, stride=2), :]
-            odds = grid[p, pl.ds(1, half_rows, stride=2), :]
-            out[2 * p] = jnp.where(half_left, even, pltpu.roll(odds, SIDE, 1))
-            out[2 * p + 1] = jnp.where(half_left, pltpu.roll(even, SIDE, 1), odds)
-
     def out_wait(phase, ref, s):
         q = lax.rem(c + s, n)
         copy(
-            ref.at[q], ref.at[q], out_send.at[phase, 0], out_recv.at[phase, q], r, c
+            final.at[phase], lines(ref, q), out_send.at[phase, 0], out_recv.at[phase, q], r, c
         ).wait_recv()
 
-    each(1, n, lambda s: out_wait(0, image_ref, s))
-    emit(image_ref, image_out)
-    second_ref[c] = gathered(1, energy * residual.astype(F32))
-    each(1, n, lambda s: out_copy(1, second_ref, s).start())
-
-    def finish(s):
-        out_wait(1, second_ref, s)
-        for phase, ref in enumerate((image_ref, second_ref)):
-            out_copy(phase, ref, s).wait_send()
-            row_copy(phase, s).wait_send()
+    def sent(s):
+        out_copy(0, image_out, s).wait_send()
+        row_copy(0, s).wait_send()
         far_copy(v_ref.at[c], 0, s).wait_send()
         far_copy(near.at[c], 1, s).wait_send()
         near_copy(s).wait_send()
 
-    each(1, n, finish)
-
-    emit(second_ref, second_out)
+    each(1, n, sent)
     for phase in range(2):
         each(0, n, lambda q: not_me(q, lambda: col_copy(phase, q).wait_send()))
     each(1, everyone, lambda s: num_copy(s).wait_send())
+    each(1, n, lambda s: out_wait(0, image_out, s))
+    publish(1, second_out, gathered(1, energy * residual.astype(F32)))
+    each(1, n, lambda s: out_copy(1, second_out, s).start())
+
+    def finish(s):
+        out_wait(1, second_out, s)
+        out_copy(1, second_out, s).wait_send()
+        row_copy(1, s).wait_send()
+
+    each(1, n, finish)
+
+
+def store(image_ref, second_ref, image_out, second_out, sem):
+    copies = [
+        pltpu.make_async_copy(src, dst, sem.at[i])
+        for i, (src, dst) in enumerate(((image_ref, image_out), (second_ref, second_out)))
+    ]
+    for move in copies:
+        move.start()
+    for move in copies:
+        move.wait()
 
 
 def local(n, vectors, energy, tiles, tile_rows, tile_cols, counts):
@@ -381,24 +423,24 @@
     everyone = n * n
     pairs = width // LANES
     half_rows = groups // 2
+    rows = here * half_rows
     vmem = pl.BlockSpec(memory_space=pltpu.VMEM)
     hbm = pl.BlockSpec(memory_space=pltpu.HBM)
     dma = pltpu.SemaphoreType.DMA
     image, second = pl.pallas_call(
         functools.partial(kernel, n),
-        out_shape=[jax.ShapeDtypeStruct((here, half_rows, LANES), F32)] * 2,
+        out_shape=[jax.ShapeDtypeStruct((rows, LANES), F32)] * 2,
         in_specs=[pl.BlockSpec(memory_space=pltpu.SMEM)] + [hbm] * 5,
         out_specs=[vmem, vmem],
         scratch_shapes=[
-            pltpu.VMEM((here, half_rows, LANES), BF16),
+            pltpu.VMEM((rows, LANES), BF16),
             pltpu.VMEM((half_rows, LANES), F32),
             pltpu.VMEM((slots, area), BF16),
             pltpu.VMEM((1, slots), jnp.int32),
             pltpu.VMEM((1, slots), jnp.int32),
             pltpu.VMEM((n, depth, width), BF16),
-            pltpu.VMEM((pairs, groups, LANES), F32),
-            pltpu.VMEM((n, depth, width), F32),
-            pltpu.VMEM((n, depth, width), F32),
+            pltpu.VMEM((rows, LANES), F32),
+            pltpu.VMEM((2, rows // n, LANES), F32),
             pltpu.VMEM((2 * area, LANES), BF16),
             pltpu.VMEM((LANES, area), BF16),
             pltpu.VMEM((LANES, area), BF16),
@@ -418,14 +460,32 @@
             dma((5,)),
         ],
         compiler_params=pltpu.CompilerParams(
-            collective_id=0, has_side_effects=True, vmem_limit_bytes=67043328
+            collective_id=0, has_side_effects=True, vmem_limit_bytes=32 * 1024 * 1024
         ),
     )(
-        counts, vectors.reshape(here, half_rows, LANES), energy.reshape(half_rows, LANES),
-        tile_rows[0], tile_cols[0], tiles[0, 0],
+        counts,
+        *[
+            pltpu.with_memory_space_constraint(x, pltpu.HBM)
+            for x in (
+                vectors.reshape(here, half_rows, LANES).transpose(1, 0, 2).reshape(rows, LANES),
+                energy.reshape(half_rows, LANES), tile_rows[0], tile_cols[0], tiles[0, 0],
+            )
+        ]
     )
 
-    return image.reshape(here, group_width), second.reshape(here, group_width)
+    image, second = pl.pallas_call(
+        store,
+        out_shape=[jax.ShapeDtypeStruct((rows, LANES), F32)] * 2,
+        in_specs=[vmem] * 2,
+        out_specs=[hbm] * 2,
+        scratch_shapes=[dma((2,))],
+        compiler_params=pltpu.CompilerParams(vmem_limit_bytes=4 * 1024 * 1024),
+    )(image, second)
+
+    def unfold(x):
+        return x.reshape(half_rows, here, LANES).transpose(1, 0, 2).reshape(here, group_width)
+
+    return unfold(image), unfold(second)
 
 
 def solution(mesh):

time: 39.6 us -> 36.6 us (0.924)
  local copies, waits for them, and re-layouts: 3.32 us -> 0 us
  Pallas kernels: 34.8 us -> 35.2 us
    reshape x1 -> x0, local copies, waits for them, and re-layouts: 1.84 us -> none  [local(): return (image.reshape(here, group_width), second.reshape(here, group_width))]
    unnamed x1 -> x0, local copies, waits for them, and re-layouts: 1.48 us -> none
    pallas_call x0 -> x1, Pallas kernels: none -> 0.72 us  [local(): pl.pallas_call(store, out_shape=[jax.ShapeDtypeStruct((rows, LANES), F32)...]
where the time goes in v1:
time: 36.6 us; the launch traced here: 36.4 us
  Pallas kernels  35.2 us (96%)
  between operations  1.29 us (4%)
    pallas_call x1, Pallas kernels, local(): pl.pallas_call(functools.partial(kernel, n), out_shape=[jax.ShapeDtypeStr...  34.4 us

profile of v1, /device:TPU:0, one launch (start us, length us, event | category | flops | bytes accessed | tf_op | source)
XLA Modules:
  0.0 36.4 jit_solution(10308036879812321430)
XLA Ops:
  1.3 34.4 %shard_map.77 = (f32[256,128]{1,0:T(8,128)S(1)}, f32[256,128]{1,0:T(8,128)S(1)}) custom-call(s32[1,1]{1,0:T(1,128)S(6)} %copy.11.counts_ref, bf16[256,128]{1,0:T(8,128)(2,1)} %bitcast.20, f32[64,128]{1,0:T(8,128)} %bitcast.21, s32[1,192]{1,0:T(1,128)} %bitcast.22, s32[1,192]{1,0:T(1,128)} %bitcast.23, bf16[192,4096]{1,0:T(8,128)(2,1)} %bitcast.19), custom_call_target="tpu_custom_call" | custom-call | tf_op jit(solution)/shard_map/pallas_call | solution.py:430
  35.7 0.7 %shard_map.78 = (f32[256,128]{1,0:T(8,128)}, f32[256,128]{1,0:T(8,128)}) custom-call(f32[256,128]{1,0:T(8,128)S(1)} %get-tuple-element.6.image_ref, f32[256,128]{1,0:T(8,128)S(1)} %get-tuple-element.7.second_ref), custom_call_target="tpu_custom_call" | custom-call | tf_op jit(solution)/shard_map/pallas_call | solution.py:476
